TPU v7x, 512 devices: a whole 4x4x16 slice. The times are simulated.
512 devices in a mesh: mp: 2 (over x_hi), dp: 32 (over z, core), tensor: 8 (over x_lo, y).
Axes of the slice: x: 4 (x_hi: 2, x_lo: 2; x = x_hi * 2 + x_lo), y: 4, z: 16, core: 2. Of those that a mesh axis runs over, the one named last changes fastest.
Arguments:
- acts: bfloat16 [2, 1024, 8192], P('mp', 'dp', 'tensor'), may hold values from -6 to 6
- gate_w: bfloat16 [2, 8192, 28672], P('mp', 'tensor', 'dp'), may hold values from -0.0625 to 0.0625
- up_w: bfloat16 [2, 8192, 28672], P('mp', 'tensor', 'dp'), may hold values from -0.0625 to 0.0625
- panel_units: int32 [8192], replicated, may hold values from 0 to 28671, as said below
Outputs:
- score: bfloat16 [8192, 28672], P(('mp', 'tensor'), 'dp')
Inputs may be any that keep to these rules, and one draw needn't show every extreme that they name: `panel_units`: write an entry's position as ((r * 32) + b) * 16 + k with 0 <= k < 16; the entry lies in [b * 896, (b + 1) * 896), all entries are distinct, and the first and the last unit of every block are among them.
All inputs are finite; a program needn't handle non-finite values.
Results may differ from a plain program's by a relative error of at most 0.03.
Values may be sent and summed in bfloat16 or wider, within the bound.
A program may use at most 64 MiB of HBM per device.

v0:
```python
import math

import jax
import jax.numpy as jnp
from jax import lax
from jax.sharding import PartitionSpec as P

epsilon = 1e-05


def passed_along(value, axis, by):
    length = lax.axis_size(axis)
    pairs = [(i, i + by) for i in range(length) if 0 <= i + by < length]
    return lax.ppermute(value, axis, pairs)


def cross_models(full_units, panel_own, panel_next, model_index):
    other_units = passed_along(full_units, "mp", -1)
    other_panel = passed_along(panel_next, "mp", 1)
    is_first = model_index == 0
    return (
        jnp.where(is_first, panel_own, other_panel),
        jnp.where(is_first, other_units, full_units),
    )


def body(acts, gate_w, up_w, panel_units):
    model_index = lax.axis_index("mp")
    unit_block = lax.axis_index("dp")
    n_model = lax.axis_size("mp")
    n_data = lax.axis_size("dp")
    n_width = lax.axis_size("tensor")
    weight_gate = gate_w[0]
    weight_up = up_w[0]
    units = weight_gate.shape[1]
    gathered = lax.all_gather(acts[0], "dp", axis=0, tiled=True)
    tokens = gathered.shape[0]
    token_share = tokens // n_width
    score_scale = 1.0 / math.sqrt(tokens)
    panel_picks = panel_units.reshape(n_model, n_width, n_data, -1)
    panel_picks = (
        lax.dynamic_index_in_dim(panel_picks, unit_block, axis=2, keepdims=False)
        - unit_block * units
    )
    gate_part = jnp.dot(gathered, weight_gate, preferred_element_type=jnp.float32)
    up_part = jnp.dot(gathered, weight_up, preferred_element_type=jnp.float32)
    summed = lax.psum_scatter(
        jnp.concatenate([gate_part, up_part], axis=1).astype(jnp.bfloat16),
        "tensor",
        scatter_dimension=0,
        tiled=True,
    ).astype(jnp.float32)
    hidden = (jax.nn.silu(summed[:, :units]) * summed[:, units:]).astype(jnp.bfloat16)
    wide_hidden = hidden.astype(jnp.float32)
    totals = lax.psum(
        (jnp.sum(wide_hidden, axis=0), jnp.sum(wide_hidden * wide_hidden, axis=0)), "tensor"
    )
    unit_mean = totals[0] / tokens
    unit_var = totals[1] / tokens - unit_mean * unit_mean
    scored = ((wide_hidden - unit_mean) * lax.rsqrt(unit_var + epsilon)).astype(jnp.bfloat16)
    full_units = lax.all_gather(scored, "tensor", axis=0, tiled=True)
    order_list = panel_picks.transpose(1, 0, 2).reshape(-1)
    chosen = jnp.take(scored, order_list, axis=1).reshape(token_share, n_width, -1)
    moved_rows = lax.all_to_all(chosen, "tensor", split_axis=1, concat_axis=0, tiled=True)
    moved_rows = moved_rows.reshape(tokens, n_model, -1)
    panel_cols = lax.all_gather(moved_rows, "dp", axis=2, tiled=True)
    mine_a, mine_b = cross_models(full_units, panel_cols[:, 0], panel_cols[:, 1], model_index)
    result = lax.dot_general(
        mine_a, mine_b, (((0,), (0,)), ((), ())), preferred_element_type=jnp.float32
    )
    return (result * score_scale).astype(jnp.bfloat16)


def solution(mesh):
    in_specs = (P("mp", "dp", "tensor"), P("mp", "tensor", "dp"), P("mp", "tensor", "dp"), P())
    out_specs = P(("mp", "tensor"), "dp")
    return jax.shard_map(body, mesh=mesh, in_specs=in_specs, out_specs=out_specs, check_vma=False)
```

profile of v0, /device:TPU:1, one launch (start us, length us, event | category | flops | bytes accessed | tf_op | source)
XLA Modules:
  0.0 338.9 jit_solution(10605596265551672443)
XLA Ops:
  6.5 0.0 copy-start
  6.5 0.0 all-gather.9.cloned.1.call-start
  6.5 0.7 all-gather.9.cloned.1.call-update
  7.3 0.0 reduce-scatter.4.cloned.1.call-start
  7.3 79.3 %all-gather.9.cloned.1.call-done = bf16[1,1024,1024]{2,1,0:T(8,128)(2,1)} async-done(((bf16[1,32,1024]{2,1,0:T(8,128)(2,1)}), bf16[1,1024,1024]{2,1,0:T(8,128)(2,1)}) %all-gather.9.cloned.1.call-update) | async-done | bytes 2097168 | tf_op jit(solution)/shard_map/all_gather | solution.py:36
  86.6 0.0 copy-done
  86.6 0.0 copy-start.2
  86.6 0.0 copy-start.3
  86.6 3.9 %fusion.14 = bf16[1024,896]{0,1:T(8,128)(2,1)S(1)} fusion(bf16[1,1024,896]{2,1,0:T(8,128)(2,1)S(1)} %copy-done, bf16[1,1024,1024]{2,1,0:T(8,128)(2,1)} %all-gather.9.cloned.1.call-done), kind=kOutput, calls=%fused_computation.13 | convolution fusion | flops 1879965696 | bytes 5767168 | tf_op jit(solution)/shard_map/dot_general | solution.py:46
  90.5 0.0 copy-done.2
  90.5 0.0 copy-done.3
  90.5 2.1 fusion.9
  92.6 2.2 pad_maximum_fusion
  94.8 5.9 %copy.13 = bf16[1024,1792]{1,0:T(8,128)(2,1)} copy(bf16[1024,1792]{0,1:T(8,128)(2,1)} %pad_maximum_fusion) | data formatting | bytes 7340032
  100.7 0.0 reduce-scatter.4.cloned.1.call-update
  100.8 0.0 all-gather.7.cloned.1.call-start
  100.8 50.9 %reduce-scatter.4.cloned.1.call-done = bf16[128,1792]{1,0:T(8,128)(2,1)} async-done(((bf16[1024,1792]{1,0:T(8,128)(2,1)}), bf16[128,1792]{1,0:T(8,128)(2,1)}) %reduce-scatter.4.cloned.1.call-update) | async-done | bytes 458768
  151.8 1.3 copy.14
  153.0 0.0 copy-start.1
  153.0 0.1 convert_element_type.16
  153.1 0.3 convert_reduce_fusion
  153.5 14.8 %all-reduce = (f32[896]{0:T(1024)S(1)}, f32[896]{0:T(1024)S(1)}) all-reduce(f32[896]{0:T(1024)S(1)} %get-tuple-element.6, f32[896]{0:T(1024)S(1)} %get-tuple-element.5), channel_id=1, replica_groups=mesh['mp'=2,'dp'=32,'tensor'=8] {'tensor'}, use_global_device_ids=true, to_apply=%region_4.5 | all-reduce | flops 1792 | bytes 14336 | tf_op jit(solution)/shard_map/psum | solution.py:55
  168.3 1.0 fusion.25
  169.3 0.0 all-gather.7.cloned.1.call-update
  169.3 0.0 all-gather.5.cloned.1.call-start
  169.3 0.0 copy-done.1
  169.3 0.1 reshape.57
  169.5 0.1 reshape.59
  169.6 0.1 reshape.58
  169.7 1.7 gather_fusion
  171.4 0.1 broadcast_select_fusion
  171.5 7.6 %all_to_all.15 = bf16[128,8,32]{0,2,1:T(8,128)(2,1)S(1)} all-to-all(bf16[128,8,32]{0,2,1:T(8,128)(2,1)S(1)} %broadcast_select_fusion), channel_id=1, replica_groups=mesh['mp'=2,'dp'=32,'tensor'=8] {'tensor'}, dimensions={1} | all-to-all | bytes 131072 | tf_op jit(solution)/shard_map/all_to_all | solution.py:64
  179.1 0.7 reshape.60
  179.8 0.0 all-gather.5.cloned.1.call-update
  179.8 40.3 %all-gather.7.cloned.1.call-done = bf16[1024,896]{0,1:T(8,128)(2,1)} async-done(((bf16[128,896]{0,1:T(8,128)(2,1)}), bf16[1024,896]{0,1:T(8,128)(2,1)}) %all-gather.7.cloned.1.call-update) | async-done | bytes 1835024 | tf_op jit(solution)/shard_map/all_gather | solution.py:61
  220.1 1.3 collective-permute-start.1
  221.4 78.8 %all-gather.5.cloned.1.call-done = bf16[1024,2,512]{0,2,1:T(8,128)(2,1)} async-done(((bf16[1024,2,16]{0,2,1:T(8,128)(2,1)}), bf16[1024,2,512]{0,2,1:T(8,128)(2,1)}) %all-gather.5.cloned.1.call-update) | async-done | bytes 2097168 | tf_op jit(solution)/shard_map/all_gather | solution.py:66
  300.2 1.3 slice_bitcast_fusion
  301.4 5.6 %collective-permute-start = (bf16[1024,512]{0,1:T(8,128)(2,1)S(1)}, bf16[1024,512]{0,1:T(8,128)(2,1)}, u32[]{:S(2)}, u32[]{:S(2)}) collective-permute-start(bf16[1024,512]{0,1:T(8,128)(2,1)S(1)} %slice_bitcast_fusion), channel_id=1, source_target_pairs={{0,256},{1,257},{2,258},{3,259},{4,260},{5,261},{6,262},{7,263},{8... | collective-permute-start | bytes 3145736 | tf_op jit(solution)/shard_map/ppermute | solution.py:14
  307.1 0.0 collective-permute-done.1
  307.1 21.2 %collective-permute-done = bf16[1024,512]{0,1:T(8,128)(2,1)} collective-permute-done((bf16[1024,512]{0,1:T(8,128)(2,1)S(1)}, bf16[1024,512]{0,1:T(8,128)(2,1)}, u32[]{:S(2)}, u32[]{:S(2)}) %collective-permute-start) | collective-permute-done | bytes 1048608 | tf_op jit(solution)/shard_map/ppermute | solution.py:14
  328.3 4.0 %multiply_convert_fusion = bf16[512,896]{1,0:T(8,128)(2,1)} fusion(bf16[1024,896]{0,1:T(8,128)(2,1)} %collective-permute-done.1, bf16[1024,896]{0,1:T(8,128)(2,1)} %all-gather.7.cloned.1.call-done, pred[]{:T(512)S(6)} %eq.3, bf16[1024,512]{0,1:T(8,128)(2,1)} %collective-permute-done, bf16[1024,2,512]{0,2,1:T(8,128)(2,1)} %all-gather.5.cloned.1.call-done), kind=kOutput, calls=%fused_computation.8 | convolution fusion | flops 941883392 | bytes 6685696 | tf_op jit(solution)/shard_map/dot_general | solution.py:68
  (7 shorter events, 0.1 us)
Async XLA Ops:
  6.5 80.1 %copy-start = (bf16[1,1024,896]{2,1,0:T(8,128)(2,1)S(1)}, bf16[1,1024,896]{2,1,0:T(8,128)(2,1)}, u32[]{:S(2)}) copy-start(bf16[1,1024,896]{2,1,0:T(8,128)(2,1)} %param.6) | copy-start | bytes 5505028
  6.5 80.1 %all-gather.9.cloned.1.call-start = ((), (), s32[]{:S(2)}) async-start(), calls=%async_computation.4 | async-start | bytes 2162688 | tf_op jit(solution)/shard_map/all_gather | solution.py:36
  7.3 144.5 %reduce-scatter.4.cloned.1.call-start = ((), (), s32[]{:S(2)}) async-start(), calls=%async_computation.5 | async-start | bytes 4128768
  86.6 3.9 %copy-start.2 = (bf16[1,1024,1024]{2,1,0:T(8,128)(2,1)S(1)}, bf16[1,1024,1024]{2,1,0:T(8,128)(2,1)}, u32[]{:S(2)}) copy-start(bf16[1,1024,1024]{2,1,0:T(8,128)(2,1)} %all-gather.9.cloned.1.call-done) | copy-start | bytes 6291460
  86.6 3.9 %copy-start.3 = (bf16[1,1024,896]{2,1,0:T(8,128)(2,1)S(1)}, bf16[1,1024,896]{2,1,0:T(8,128)(2,1)}, u32[]{:S(2)}) copy-start(bf16[1,1024,896]{2,1,0:T(8,128)(2,1)} %param.5) | copy-start | bytes 5505028
  100.8 119.3 %all-gather.7.cloned.1.call-start = ((), (), s32[]{:S(2)}) async-start(), calls=%async_computation.3 | async-start | bytes 2064384 | tf_op jit(solution)/shard_map/all_gather | solution.py:61
  153.0 16.3 %copy-start.1 = (s32[8192]{0:T(1024)S(1)}, s32[8192]{0:T(1024)}, u32[]{:S(2)}) copy-start(s32[8192]{0:T(1024)} %param.7) | copy-start | bytes 98308
  169.3 130.9 %all-gather.5.cloned.1.call-start = ((), (), s32[]{:S(2)}) async-start(), calls=%async_computation.2 | async-start | bytes 2162688 | tf_op jit(solution)/shard_map/all_gather | solution.py:66
  220.1 87.0 %collective-permute-start.1 = (bf16[1024,896]{0,1:T(8,128)(2,1)}, bf16[1024,896]{0,1:T(8,128)(2,1)}, u32[]{:S(2)}, u32[]{:S(2)}) collective-permute-start(bf16[1024,896]{0,1:T(8,128)(2,1)} %all-gather.7.cloned.1.call-done), channel_id=1, source_target_pairs={{256,0},{257,1},{258,2},{259,3},{260,4},{261,5},{262,6},{263,7},{2... | collective-permute-start | bytes 5505032 | tf_op jit(solution)/shard_map/ppermute | solution.py:14
  301.4 26.9 %collective-permute-start = (bf16[1024,512]{0,1:T(8,128)(2,1)S(1)}, bf16[1024,512]{0,1:T(8,128)(2,1)}, u32[]{:S(2)}, u32[]{:S(2)}) collective-permute-start(bf16[1024,512]{0,1:T(8,128)(2,1)S(1)} %slice_bitcast_fusion), channel_id=1, source_target_pairs={{0,256},{1,257},{2,258},{3,259},{4,260},{5,261},{6,262},{7,263},{8... | collective-permute-start | bytes 3145736 | tf_op jit(solution)/shard_map/ppermute | solution.py:14
Sparse Core Ops, SparseCore 0:
  9.5 77.1 all-gather.8
  100.9 50.8 reduce-scatter.3
  169.4 50.6 all-gather.6
  222.1 78.0 all-gather.4
where the time goes:
time: 340 us; the launch traced here: 339 us
  waiting for transfers between devices  271 us (80%)
  blocking collectives  22.4 us (7%)
  between operations  13.3 us (4%)
  local copies, waits for them, and re-layouts  11.2 us (3%)
  matrix products  10 us (3%)
  starting transfers between devices  7.05 us (2%)
  other arithmetic  3.74 us (1%)
    all_gather x1, waiting for transfers between devices, body(): gathered = lax.all_gather(acts[0], 'dp', axis=0, tiled=True)  79.3 us
    all_gather x1, waiting for transfers between devices, body(): panel_cols = lax.all_gather(moved_rows, 'dp', axis=2, tiled=True)  78.8 us
    unnamed x5, waiting for transfers between devices  51.7 us
    all_gather x1, waiting for transfers between devices, body(): full_units = lax.all_gather(scored, 'tensor', axis=0, tiled=True)  40.3 us
    ppermute x2, waiting for transfers between devices, passed_along(): return lax.ppermute(value, axis, pairs)  21.2 us
    psum x1, blocking collectives, body(): lax.psum((jnp.sum(wide_hidden, axis=0), jnp.sum(wide_hidden * wide_hidden...  14.8 us
    all_to_all x1, blocking collectives, body(): lax.all_to_all(chosen, 'tensor', split_axis=1, concat_axis=0, tiled=True)  7.58 us
    unnamed x10, local copies, waits for them, and re-layouts  7.23 us
  transfers between devices with their start and end apart: 6, of which 5 were waited for; matrix products, arithmetic and copies ran while one was open for 1% of the time, Pallas kernels for 0%

commit v1 on v0

v1 whole, which is shorter than its diff:
```python
import functools
import math

import jax
import jax.numpy as jnp
from jax import lax
from jax.experimental import pallas as pl
from jax.experimental.pallas import tpu as pltpu
from jax.sharding import PartitionSpec as P

MESH = pl.DeviceIdType.MESH
F32 = jnp.float32
BF16 = jnp.bfloat16
EPS = 1e-05
TILE = 16
PICK = 16


def wrap(value, n):
    return lax.rem(value + n, n)


def remote(src, dst, send_sem, recv_sem, device):
    return pltpu.make_async_remote_copy(
        src_ref=src,
        dst_ref=dst,
        send_sem=send_sem,
        recv_sem=recv_sem,
        device_id=device,
        device_id_type=MESH,
    )


def silu_times(gate, up):
    return (gate / (1.0 + jnp.exp(-gate)) * up).astype(BF16)


def kernel(
    n_data, n_width, acts_ref, gate_ref, up_ref, table_ref, out_ref,
    xbuf, wg, wu, part_b, got_b, hid_b, sel_w, part_a, got_a, cross_z, panel,
    load_sem, up_s, up_r, dn_s, dn_r, pt_s, pt_r, rs_s, rs_r, ag_s, ag_r,
    xc_s, xc_r, ra_s, ra_r, cz_s, cz_r,
):
    mp = lax.axis_index("mp")
    dp = lax.axis_index("dp")
    t = lax.axis_index("tensor")
    chip = dp // 2
    core = lax.rem(dp, 2)
    n_chip = n_data // 2
    half = n_chip // 2
    rows = acts_ref.shape[1]
    width = acts_ref.shape[2]
    units = gate_ref.shape[2]
    tokens = n_data * rows
    nxt = {"dp": wrap(dp + 2, n_data)}
    prv = {"dp": wrap(dp - 2, n_data)}
    mate_dp = dp + 1 - 2 * core
    mate = {"dp": mate_dp}
    other = {"mp": 1 - mp}
    is_a = mp == 0
    is_b = mp == 1

    def peer_of(d):
        return lax.rem(t + d, n_width)

    loads = [
        pltpu.make_async_copy(acts_ref.at[0], xbuf.at[dp], load_sem.at[0]),
        pltpu.make_async_copy(gate_ref.at[0], wg, load_sem.at[1]),
        pltpu.make_async_copy(up_ref.at[0], wu, load_sem.at[2]),
    ]
    for load in loads:
        load.start()

    barrier = pltpu.get_barrier_semaphore()
    greeted = [nxt, prv, mate, other] + [{"tensor": peer_of(d)} for d in range(1, n_width)]
    for device in greeted:
        pl.semaphore_signal(barrier, inc=1, device_id=device, device_id_type=MESH)
    pl.semaphore_wait(barrier, len(greeted))

    def ring_start(buf, k):
        own = buf.at[dp]
        remote(own, own, up_s.at[k, 1], up_r.at[k, 1], nxt).start()
        remote(own, own, dn_s.at[k, 1], dn_r.at[k, 1], prv).start()
        remote(own, own, pt_s.at[k, 0], pt_r.at[k, 0], mate).start()

    def ring_mate_own(buf, k):
        theirs = buf.at[mate_dp]
        remote(theirs, theirs, pt_s.at[k, 0], pt_r.at[k, 0], mate).wait_recv()

    sides = ((-2, 0, up_s, up_r, nxt, 0), (2, 1, dn_s, dn_r, prv, 1))

    def ring_step(buf, k, s):
        for step, last_core, ss, rs, device, odd in sides:
            @pl.when((s < half) | (core == last_core))
            def _():
                ref = buf.at[wrap(dp + step * s, n_data)]
                remote(ref, ref, ss.at[k, s], rs.at[k, s], device).wait_recv()

                @pl.when((s + 1 < half) | ((s + 1 == half) & (core == last_core)))
                def _():
                    remote(ref, ref, ss.at[k, s + 1], rs.at[k, s + 1], device).start()

                slot = 2 * s + odd
                remote(ref, ref, pt_s.at[k, slot], pt_r.at[k, slot], mate).start()

    def ring_mate(buf, k, s):
        for step, last_core, _ss, _rs, _device, odd in sides:
            @pl.when((s < half) | (core != last_core))
            def _():
                ref = buf.at[wrap(mate_dp + step * s, n_data)]
                slot = 2 * s + odd
                remote(ref, ref, pt_s.at[k, slot], pt_r.at[k, slot], mate).wait_recv()

    def ring_drain(buf, k):
        own = buf.at[dp]
        remote(own, own, pt_s.at[k, 0], pt_r.at[k, 0], mate).wait_send()

        def body(s, carry):
            for _step, last_core, ss, rs, device, odd in sides:
                @pl.when((s < half) | (core == last_core))
                def _():
                    slot = 2 * s + odd
                    remote(own, own, ss.at[k, s], rs.at[k, s], device).wait_send()
                    remote(own, own, pt_s.at[k, slot], pt_r.at[k, slot], mate).wait_send()
            return carry

        lax.fori_loop(1, half + 1, body, 0)

    def chips_of(s):
        return wrap(chip - s, n_chip), lax.rem(chip + lax.rem(s, half), n_chip)

    def tile_of(s, who):
        low, high = chips_of(s)
        quarter = n_width // 2
        return jnp.where(who < quarter, low, high) * quarter + lax.rem(who, quarter)

    def spread(s):
        ref = hid_b.at[tile_of(s, t)]
        for d in range(1, n_width):
            peer = peer_of(d)
            remote(ref, ref, ag_s.at[s - 1, peer], ag_r.at[s - 1, t], {"tensor": peer}).start()

    def b_product(s):
        low, high = chips_of(s)
        x = jnp.concatenate(
            [xbuf[2 * low], xbuf[2 * low + 1], xbuf[2 * high], xbuf[2 * high + 1]], axis=0
        )
        for weight, start in ((wg, 0), (wu, units)):
            y = jnp.dot(x, weight[...], preferred_element_type=F32).astype(BF16)
            part_b[s - 1, :, :, start:start + units] = y.reshape(n_width, TILE, units)
        for d in range(1, n_width):
            peer = peer_of(d)
            remote(
                part_b.at[s - 1, peer], got_b.at[s - 1, t],
                rs_s.at[s - 1, peer], rs_r.at[s - 1, t], {"tensor": peer},
            ).start()

    def b_sum(s):
        total = part_b[s - 1, t].astype(F32)
        for d in range(1, n_width):
            src = peer_of(d)
            ref = got_b.at[s - 1, src]
            remote(ref, ref, rs_s.at[s - 1, src], rs_r.at[s - 1, src], {"tensor": src}).wait_recv()
            total = total + got_b[s - 1, src].astype(F32)
        tile = tile_of(s, t)
        hid_b[tile] = silu_times(total[:, :units], total[:, units:])
        ref = hid_b.at[tile]
        remote(ref, ref, xc_s.at[s - 1], xc_r.at[s - 1], other).start()
        spread(s)

    def a_select():
        blocks_row = n_data // 8
        found = table_ref[pl.ds(dp // 8, 2 * n_width, stride=blocks_row), :]
        found = jnp.broadcast_to(found[:, None, :], (2 * n_width, PICK, 128))
        found = found.reshape(2 * n_width * PICK, 128)
        shape = found.shape
        lane = lax.broadcasted_iota(jnp.int32, shape, 1)
        pick = lax.rem(lax.broadcasted_iota(jnp.int32, shape, 0), PICK)
        wanted = lax.rem(dp, 8) * PICK + pick
        local = jnp.where(lane == wanted, found - dp * units, 0).astype(F32)
        column = jnp.sum(local, axis=1, keepdims=True).astype(jnp.int32)
        unit = lax.broadcasted_iota(jnp.int32, (shape[0], units), 1)
        chosen = jnp.where(unit == column, 1.0, 0.0).astype(BF16)
        for i, weight in enumerate((wg, wu)):
            sel_w[i] = lax.dot_general(
                chosen, weight[...], (((1,), (1,)), ((), ())), preferred_element_type=F32
            ).astype(BF16)

    def a_product():
        span = 4 * 2 * rows

        def body(i, carry):
            blocks = span // rows
            x = xbuf[pl.ds(i * blocks, blocks)].reshape(span, width)
            columns = pl.ds(pl.multiple_of(i * span, span), span)
            for kind in range(2):
                y = lax.dot_general(
                    sel_w[kind], x, (((1,), (1,)), ((), ())), preferred_element_type=F32
                ).astype(BF16)
                for r in range(2 * n_width):
                    part_a[r // n_width, r % n_width, kind, :, columns] = y[r * PICK:(r + 1) * PICK]
            return carry

        lax.fori_loop(0, tokens // span, body, 0)
        for d in range(1, n_width):
            peer = peer_of(d)
            remote(
                part_a.at[:, peer], got_a.at[t], ra_s.at[peer], ra_r.at[t], {"tensor": peer}
            ).start()

    def a_sum():
        for d in range(1, n_width):
            src = peer_of(d)
            ref = got_a.at[src]
            remote(ref, ref, ra_s.at[src], ra_r.at[src], {"tensor": src}).wait_recv()
        for group in (1, 0):
            gate = part_a[group, t, 0].astype(F32)
            up = part_a[group, t, 1].astype(F32)
            for d in range(1, n_width):
                gate = gate + got_a[peer_of(d), group, 0].astype(F32)
                up = up + got_a[peer_of(d), group, 1].astype(F32)
            wide = silu_times(gate, up).astype(F32)
            mean = jnp.sum(wide, axis=1, keepdims=True) / tokens
            var = jnp.sum(wide * wide, axis=1, keepdims=True) / tokens - mean * mean
            z = ((wide - mean) * lax.rsqrt(var + EPS)).astype(BF16)
            if group == 1:
                cross_z[...] = z
                remote(cross_z, panel.at[dp], cz_s.at[0], cz_r.at[0], other).start()
            else:
                panel[dp] = z

    loads[0].wait()
    ring_start(xbuf, 0)
    loads[1].wait()
    loads[2].wait()

    @pl.when(is_a)
    def _():
        a_select()

    ring_mate_own(xbuf, 0)

    def gather_step(s, carry):
        ring_step(xbuf, 0, s)
        ring_mate(xbuf, 0, s)

        @pl.when(is_b)
        def _():
            b_product(s)

        return carry

    lax.fori_loop(1, half + 1, gather_step, 0)

    @pl.when(is_a)
    def _():
        a_product()
        a_sum()
        ring_start(panel, 1)

        def step(s, carry):
            ring_step(panel, 1, s)
            ring_mate(panel, 1, s)
            ref = hid_b.at[tile_of(s, t)]
            remote(ref, ref, xc_s.at[s - 1], xc_r.at[s - 1], other).wait_recv()
            spread(s)
            return carry

        lax.fori_loop(1, half + 1, step, 0)

    @pl.when(is_b)
    def _():
        def early(s, carry):
            b_sum(s)
            return carry

        lax.fori_loop(1, half // 2 + 1, early, 0)
        own = panel.at[dp]
        remote(own, own, cz_s.at[0], cz_r.at[0], other).wait_recv()
        ring_start(panel, 1)

        def late(s, carry):
            b_sum(half // 2 + s)
            for j in (2 * s - 1, 2 * s):
                ring_step(panel, 1, j)
                ring_mate(panel, 1, j)
            return carry

        lax.fori_loop(1, half // 2 + 1, late, 0)

    ring_mate_own(panel, 1)

    def arrive(s, carry):
        for d in range(1, n_width):
            src = peer_of(d)
            ref = hid_b.at[tile_of(s, src)]
            remote(ref, ref, ag_s.at[s - 1, src], ag_r.at[s - 1, src], {"tensor": src}).wait_recv()
        return carry

    lax.fori_loop(1, half + 1, arrive, 0)

    left = panel[...].reshape(n_data * PICK, tokens)
    scale = 1.0 / math.sqrt(tokens)
    start = 0
    while start < units:
        size = min(256, units - start)
        wide = hid_b[:, :, start:start + size].reshape(tokens, size).astype(F32)
        mean = jnp.sum(wide, axis=0, keepdims=True) / tokens
        var = jnp.sum(wide * wide, axis=0, keepdims=True) / tokens - mean * mean
        z = ((wide - mean) * lax.rsqrt(var + EPS)).astype(BF16)
        score = jnp.dot(left, z, preferred_element_type=F32) * scale
        out_ref[:, start:start + size] = score.astype(BF16)
        start += size

    ring_drain(xbuf, 0)
    ring_drain(panel, 1)

    def sent(s, carry):
        for d in range(1, n_width):
            peer = peer_of(d)
            ref = hid_b.at[tile_of(s, t)]
            remote(ref, ref, ag_s.at[s - 1, peer], ag_r.at[s - 1, t], {"tensor": peer}).wait_send()

            @pl.when(is_b)
            def _():
                src = part_b.at[s - 1, peer]
                remote(src, src, rs_s.at[s - 1, peer], rs_r.at[s - 1, t], {"tensor": peer}).wait_send()

        @pl.when(is_b)
        def _():
            mine = hid_b.at[tile_of(s, t)]
            remote(mine, mine, xc_s.at[s - 1], xc_r.at[s - 1], other).wait_send()

        return carry

    lax.fori_loop(1, half + 1, sent, 0)

    @pl.when(is_a)
    def _():
        remote(cross_z, panel.at[dp], cz_s.at[0], cz_r.at[0], other).wait_send()
        for d in range(1, n_width):
            peer = peer_of(d)
            remote(
                part_a.at[:, peer], got_a.at[t], ra_s.at[peer], ra_r.at[t], {"tensor": peer}
            ).wait_send()


def body(n_data, n_width, acts, gate_w, up_w, panel_units):
    _, rows, width = acts.shape
    units = gate_w.shape[2]
    tokens = n_data * rows
    steps = n_data // 4
    any_space = pl.BlockSpec(memory_space=pl.ANY)
    vmem = pl.BlockSpec(memory_space=pltpu.VMEM)
    dma = pltpu.SemaphoreType.DMA
    return pl.pallas_call(
        functools.partial(kernel, n_data, n_width),
        out_shape=jax.ShapeDtypeStruct((n_data * PICK, units), BF16),
        in_specs=[any_space, any_space, any_space, vmem],
        out_specs=vmem,
        scratch_shapes=[
            pltpu.VMEM((n_data, rows, width), BF16),
            pltpu.VMEM((width, units), BF16),
            pltpu.VMEM((width, units), BF16),
            pltpu.VMEM((steps, n_width, TILE, 2 * units), BF16),
            pltpu.VMEM((steps, n_width, TILE, 2 * units), BF16),
            pltpu.VMEM((tokens // TILE, TILE, units), BF16),
            pltpu.VMEM((2, 2 * n_width * PICK, width), BF16),
            pltpu.VMEM((2, n_width, 2, PICK, tokens), BF16),
            pltpu.VMEM((n_width, 2, 2, PICK, tokens), BF16),
            pltpu.VMEM((PICK, tokens), BF16),
            pltpu.VMEM((n_data, PICK, tokens), BF16),
            dma((3,)),
            dma((2, steps + 1)),
            dma((2, steps + 1)),
            dma((2, steps + 1)),
            dma((2, steps + 1)),
            dma((2, 2 * steps + 2)),
            dma((2, 2 * steps + 2)),
            dma((steps, n_width)),
            dma((steps, n_width)),
            dma((steps, n_width)),
            dma((steps, n_width)),
            dma((steps,)),
            dma((steps,)),
            dma((n_width,)),
            dma((n_width,)),
            dma((1,)),
            dma((1,)),
        ],
        compiler_params=pltpu.CompilerParams(
            collective_id=0, has_side_effects=True, vmem_limit_bytes=60 * 1024 * 1024
        ),
    )(acts, gate_w, up_w, panel_units.reshape(-1, 128))


def solution(mesh):
    in_specs = (P("mp", "dp", "tensor"), P("mp", "tensor", "dp"), P("mp", "tensor", "dp"), P())
    out_specs = P(("mp", "tensor"), "dp")
    step = functools.partial(body, mesh.shape["dp"], mesh.shape["tensor"])
    return jax.shard_map(step, mesh=mesh, in_specs=in_specs, out_specs=out_specs, check_vma=False)
```

time: 340 us -> 102 us (0.30)
  waiting for transfers between devices: 271 us -> 0 us
  Pallas kernels: 0 us -> 99.6 us
  blocking collectives: 22.4 us -> 0 us
  between operations: 13.3 us -> 0.01 us
  matrix products: 10 us -> 0 us
  local copies, waits for them, and re-layouts: 11.2 us -> 2.18 us
  starting transfers between devices: 7.05 us -> 0 us
  other arithmetic: 3.74 us -> 0 us
    all_gather x3 -> x0, waiting for transfers between devices: 198 us -> none  [the longest x1 79.3 us: body(): gathered = lax.all_gather(acts[0], 'dp', axis=0, tiled=True)]
    pallas_call x0 -> x1, Pallas kernels: none -> 99.6 us  [body(): pl.pallas_call(functools.partial(kernel, n_data, n_width), out_shape=jax....]
    unnamed x5 -> x0, waiting for transfers between devices: 51.7 us -> none
    ppermute x2 -> x0, waiting for transfers between devices: 21.2 us -> none  [passed_along(): return lax.ppermute(value, axis, pairs)]
    psum x1 -> x0, blocking collectives: 14.8 us -> none  [body(): lax.psum((jnp.sum(wide_hidden, axis=0), jnp.sum(wide_hidden * wide_hidden...]
    dot_general x3 -> x0, matrix products: 10 us -> none  [the longest x1 4.05 us: body(): lax.dot_general(mine_a, mine_b, (((0,), (0,)), ((), ())), preferred_eleme...]
    all_to_all x1 -> x0, blocking collectives: 7.58 us -> none  [body(): lax.all_to_all(chosen, 'tensor', split_axis=1, concat_axis=0, tiled=True)]
    ppermute x2 -> x0, starting transfers between devices: 6.92 us -> none  [passed_along(): return lax.ppermute(value, axis, pairs)]
  transfers between devices with their start and end apart: 6 -> 0, of which waited for: 5 -> 0; matrix products, arithmetic and copies ran while one was open for 1% -> 0% of each run, Pallas kernels for 0% -> 0%
where the time goes in v1:
time: 102 us
  Pallas kernels  99.6 us (98%)
  local copies, waits for them, and re-layouts  2.18 us (2%)
    pallas_call x1, Pallas kernels, body(): pl.pallas_call(functools.partial(kernel, n_data, n_width), out_shape=jax....  99.6 us
    unnamed x1, local copies, waits for them, and re-layouts  2.18 us

profile of v1, /device:TPU:1, one launch (start us, length us, event | category | flops | bytes accessed | tf_op | source)
XLA Modules:
  0.0 101.8 jit_solution(9192068144762993615)
XLA Ops:
  0.0 99.6 %shard_map.46 = bf16[512,896]{1,0:T(8,128)(2,1)} custom-call(bf16[1,32,1024]{2,1,0:T(8,128)(2,1)} %acts_ref.1, bf16[1,1024,896]{2,1,0:T(8,128)(2,1)} %gate_ref.1, bf16[1,1024,896]{2,1,0:T(8,128)(2,1)} %up_ref.1, s32[64,128]{1,0:T(8,128)} %bitcast.1), custom_call_target="tpu_custom_call" | custom-call | tf_op jit(solution)/shard_map/pallas_call | solution.py:356
  99.6 2.2 %copy.6 = bf16[512,896]{1,0:T(8,128)(2,1)} copy(bf16[512,896]{1,0:T(8,128)(2,1)} %shard_map.46) | data formatting | bytes 1835008

commit v2 on v1

v2 whole, which is shorter than its diff:
```python
import functools
import math

import jax
import jax.numpy as jnp
from jax import lax
from jax.experimental import pallas as pl
from jax.experimental.pallas import tpu as pltpu
from jax.sharding import PartitionSpec as P

MESH = pl.DeviceIdType.MESH
F32 = jnp.float32
BF16 = jnp.bfloat16
EPS = 1e-05
TILE = 16
PICK = 16


def wrap(value, n):
    return lax.rem(value + n, n)


def remote(src, dst, send_sem, recv_sem, device):
    return pltpu.make_async_remote_copy(
        src_ref=src,
        dst_ref=dst,
        send_sem=send_sem,
        recv_sem=recv_sem,
        device_id=device,
        device_id_type=MESH,
    )


def silu_times(gate, up):
    return (gate / (1.0 + jnp.exp(-gate)) * up).astype(BF16)


def kernel(
    n_data, n_width, acts_ref, gate_ref, up_ref, table_ref, out_ref,
    xbuf, wg, wu, part_b, got_x, sum_b, got_y, hid_b, sel_w, part_a, got_a, cross_z, panel,
    load_sem, up_s, up_r, dn_s, dn_r, pt_s, pt_r, px_s, px_r, rx_s, rx_r, ry_s, ry_r,
    gx_s, gx_r, g1_s, g1_r, g2_s, g2_r, xc_s, xc_r, ra_s, ra_r, cz_s, cz_r,
):
    mp = lax.axis_index("mp")
    dp = lax.axis_index("dp")
    t = lax.axis_index("tensor")
    chip = dp // 2
    core = lax.rem(dp, 2)
    n_chip = n_data // 2
    half = n_chip // 2
    reach = half // 2
    n_pair = n_chip // 2
    n_y = n_width // 2
    x = t // n_y
    y = lax.rem(t, n_y)
    rows = acts_ref.shape[1]
    width = acts_ref.shape[2]
    units = gate_ref.shape[2]
    tokens = n_data * rows
    nxt = {"dp": wrap(dp + 2, n_data)}
    prv = {"dp": wrap(dp - 2, n_data)}
    mate_dp = dp + 1 - 2 * core
    mate = {"dp": mate_dp}
    across_t = lax.rem(t + n_y, n_width)
    across = {"tensor": across_t}
    other = {"mp": 1 - mp, "tensor": across_t}
    is_a = mp == 0
    is_b = mp == 1

    helped = [s for s in (1, 3) if s <= half]

    def is_helped(s):
        return functools.reduce(jnp.logical_or, [s == h for h in helped])

    def is_owner(s):
        return jnp.logical_not(jnp.logical_xor(is_a, is_helped(s)))

    def mine(s):
        return jnp.where(is_owner(s), t, across_t)

    def theirs(s):
        return jnp.where(is_owner(s), across_t, t)

    def peer_of(d):
        return lax.rem(t + d, n_width)

    def y_of(d):
        return lax.rem(y + d, n_y)

    def at_y(row):
        return {"tensor": x * n_y + row}

    loads = [
        pltpu.make_async_copy(acts_ref.at[0], xbuf.at[dp], load_sem.at[0]),
        pltpu.make_async_copy(gate_ref.at[0], wg, load_sem.at[1]),
        pltpu.make_async_copy(up_ref.at[0], wu, load_sem.at[2]),
    ]
    for load in loads:
        load.start()

    barrier = pltpu.get_barrier_semaphore()
    greeted = [mate, other] + [{"tensor": peer_of(d)} for d in range(1, n_width)]
    for d in range(1, reach + 1):
        greeted += [{"dp": wrap(dp + 2 * d, n_data)}, {"dp": wrap(dp - 2 * d, n_data)}]
    for device in greeted:
        pl.semaphore_signal(barrier, inc=1, device_id=device, device_id_type=MESH)
    pl.semaphore_wait(barrier, len(greeted))

    sides = ((-2, 0, up_s, up_r, nxt, 0), (2, 1, dn_s, dn_r, prv, 1))
    acts_ring = (xbuf, tuple((k, pl.ds(k * TILE, TILE)) for k in range(rows // TILE)))
    spread = rows // TILE

    def ring_start(ring):
        buf, pieces = ring
        for k, part in pieces:
            own = buf.at[dp, part]
            for _step, _last, ss, rs, device, _odd in sides:
                remote(own, own, ss.at[k, 1], rs.at[k, 1], device).start()
            remote(own, own, pt_s.at[k, 0], pt_r.at[k, 0], mate).start()

    def ring_mate_own(ring):
        buf, pieces = ring
        for k, part in pieces:
            theirs = buf.at[mate_dp, part]
            remote(theirs, theirs, pt_s.at[k, 0], pt_r.at[k, 0], mate).wait_recv()

    def ring_step(ring, s):
        buf, pieces = ring
        for k, part in pieces:
            for step, last_core, ss, rs, device, odd in sides:
                @pl.when((s < half) | (core == last_core))
                def _():
                    ref = buf.at[wrap(dp + step * s, n_data), part]
                    remote(ref, ref, ss.at[k, s], rs.at[k, s], device).wait_recv()

                    @pl.when((s + 1 < half) | ((s + 1 == half) & (core == last_core)))
                    def _():
                        remote(ref, ref, ss.at[k, s + 1], rs.at[k, s + 1], device).start()

                    slot = 2 * s + odd
                    remote(ref, ref, pt_s.at[k, slot], pt_r.at[k, slot], mate).start()

    def ring_mate(ring, s):
        buf, pieces = ring
        for k, part in pieces:
            for step, last_core, _ss, _rs, _device, odd in sides:
                @pl.when((s < half) | (core != last_core))
                def _():
                    ref = buf.at[wrap(mate_dp + step * s, n_data), part]
                    slot = 2 * s + odd
                    remote(ref, ref, pt_s.at[k, slot], pt_r.at[k, slot], mate).wait_recv()

    def ring_drain(buf, pieces):
        for k, part in pieces:
            own = buf.at[dp, part]
            remote(own, own, pt_s.at[k, 0], pt_r.at[k, 0], mate).wait_send()

            def body(s, carry):
                for _step, last_core, ss, rs, device, odd in sides:
                    @pl.when((s < half) | (core == last_core))
                    def _():
                        slot = 2 * s + odd
                        remote(own, own, ss.at[k, s], rs.at[k, s], device).wait_send()
                        remote(own, own, pt_s.at[k, slot], pt_r.at[k, slot], mate).wait_send()
                return carry

            lax.fori_loop(1, half + 1, body, 0)

    def panel_start():
        own = panel.at[dp]
        for d in range(reach, 0, -1):
            for step, _last, ss, rs, _device, _odd in sides:
                target = {"dp": wrap(dp - step * d, n_data)}
                remote(own, own, ss.at[spread, d], rs.at[spread, d], target).start()
        remote(own, own, pt_s.at[spread, 0], pt_r.at[spread, 0], mate).start()

    def panel_take(d, side):
        step, _last, ss, rs, device, odd = side
        ref = panel.at[wrap(dp + step * d, n_data)]
        remote(ref, ref, ss.at[spread, d], rs.at[spread, d], device).wait_recv()
        return ref, remote(
            ref, ref, pt_s.at[spread, 2 * d + odd], pt_r.at[spread, 2 * d + odd], mate
        )

    def panel_take_own():
        own = panel.at[dp]
        remote(own, own, cz_s.at[0], cz_r.at[0], other).wait_recv()

    def panel_forward():
        for side in sides:
            step, last_core, ss, rs, _device, _odd = side
            ref, to_mate = panel_take(reach, side)

            def pass_to(d):
                target = {"dp": wrap(dp - step * d, n_data)}
                return remote(ref, ref, ss.at[spread, reach + d], rs.at[spread, reach + d], target)

            @pl.when(core == last_core)
            def _():
                pass_to(reach).start()

            for d in range(reach - 1, 0, -1):
                pass_to(d).start()
            to_mate.start()

    def panel_collect():
        for d in range(1, half + 1):
            if d == reach:
                continue
            for side in sides:
                if d < half:
                    panel_take(d, side)[1].start()
                else:
                    @pl.when(core == side[1])
                    def _():
                        panel_take(d, side)[1].start()

    def panel_mate():
        theirs = panel.at[mate_dp]
        remote(theirs, theirs, pt_s.at[spread, 0], pt_r.at[spread, 0], mate).wait_recv()

        def body(d, carry):
            for step, last_core, _ss, _rs, _device, odd in sides:
                @pl.when((d < half) | (core != last_core))
                def _():
                    ref = panel.at[wrap(mate_dp + step * d, n_data)]
                    slot = 2 * d + odd
                    remote(
                        ref, ref, pt_s.at[spread, slot], pt_r.at[spread, slot], mate
                    ).wait_recv()
            return carry

        lax.fori_loop(1, half + 1, body, 0)

    def tile_of(s, who):
        low, high = wrap(chip - s, n_chip), lax.rem(chip + lax.rem(s, half), n_chip)
        return jnp.where(who < n_y, low, high) * n_y + lax.rem(who, n_y)

    def own_copies(s):
        ref = hid_b.at[tile_of(s, mine(s))]
        copies = [remote(ref, ref, gx_s.at[s - 1], gx_r.at[s - 1], across)]
        for d in range(1, n_y):
            row = y_of(d)
            copies.append(remote(ref, ref, g1_s.at[s - 1, row], g1_r.at[s - 1, y], at_y(row)))
        return copies

    def passed_copies(s):
        ref = hid_b.at[tile_of(s, theirs(s))]
        return [
            remote(ref, ref, g2_s.at[s - 1, y_of(d)], g2_r.at[s - 1, y], at_y(y_of(d)))
            for d in range(1, n_y)
        ]

    def direct_copies(s):
        ref = hid_b.at[tile_of(s, mine(s))]
        return [
            remote(
                ref, ref, g2_s.at[s - 1, y_of(d)], g2_r.at[s - 1, y],
                {"tensor": (1 - x) * n_y + y_of(d)},
            )
            for d in range(1, n_y)
        ]

    def cross_copy(s, who):
        ref = hid_b.at[tile_of(s, who)]
        return remote(ref, ref, xc_s.at[s - 1], xc_r.at[s - 1], other)

    def pass_on(s):
        ref = hid_b.at[tile_of(s, theirs(s))]
        remote(ref, ref, gx_s.at[s - 1], gx_r.at[s - 1], across).wait_recv()
        for copy in passed_copies(s):
            copy.start()

    def x_copy(s):
        return remote(
            part_b.at[s - 1, pl.ds((1 - x) * n_y, n_y)], got_x.at[s - 1],
            rx_s.at[s - 1], rx_r.at[s - 1], across,
        )

    def raw_copy(s):
        ref = part_b.at[s - 1]
        return remote(ref, ref, px_s.at[s - 1], px_r.at[s - 1], other)

    def raw(s):
        raw_copy(s).wait_recv()
        x_copy(s).start()

    def y_copy(s, row):
        return remote(
            sum_b.at[s - 1, row], got_y.at[s - 1, y], ry_s.at[s - 1, row], ry_r.at[s - 1, y], at_y(row)
        )

    def b_product(s):
        low, high = wrap(chip - s, n_chip), lax.rem(chip + lax.rem(s, half), n_chip)
        left = jnp.concatenate(
            [xbuf[2 * low], xbuf[2 * low + 1], xbuf[2 * high], xbuf[2 * high + 1]], axis=0
        )
        for weight, start in ((wg, 0), (wu, units)):
            part = jnp.dot(left, weight[...], preferred_element_type=F32).astype(BF16)
            part_b[s - 1, :, :, start:start + units] = part.reshape(n_width, TILE, units)
        @pl.when(is_helped(s))
        def _():
            raw_copy(s).start()

        @pl.when(jnp.logical_not(is_helped(s)))
        def _():
            x_copy(s).start()

    def b_pair(s):
        x_copy(s).wait_recv()
        for d in range(1, n_y):
            row = y_of(d)
            pair = part_b[s - 1, x * n_y + row].astype(F32) + got_x[s - 1, row].astype(F32)
            sum_b[s - 1, row] = pair.astype(BF16)
            y_copy(s, row).start()

    def b_total(s):
        total = part_b[s - 1, t].astype(F32) + got_x[s - 1, y].astype(F32)
        for d in range(1, n_y):
            row = y_of(d)
            ref = got_y.at[s - 1, row]
            remote(ref, ref, ry_s.at[s - 1, row], ry_r.at[s - 1, row], at_y(row)).wait_recv()
            total = total + got_y[s - 1, row].astype(F32)
        hid_b[tile_of(s, t)] = silu_times(total[:, :units], total[:, units:])
        cross_copy(s, t).start()
        share(s)

    def share(s):
        for copy in own_copies(s):
            copy.start()

        @pl.when(is_a | (s == half))
        def _():
            for copy in direct_copies(s):
                copy.start()

    def take(s):
        cross_copy(s, mine(s)).wait_recv()
        share(s)

    def a_select():
        found = table_ref[pl.ds(dp // 8, 2 * n_width, stride=n_data // 8), :]
        found = jnp.broadcast_to(found[:, None, :], (2 * n_width, PICK, 128))
        found = found.reshape(2 * n_width * PICK, 128)
        shape = found.shape
        lane = lax.broadcasted_iota(jnp.int32, shape, 1)
        pick = lax.rem(lax.broadcasted_iota(jnp.int32, shape, 0), PICK)
        wanted = lax.rem(dp, 8) * PICK + pick
        local = jnp.where(lane == wanted, found - dp * units, 0).astype(F32)
        column = jnp.sum(local, axis=1, keepdims=True).astype(jnp.int32)
        unit = lax.broadcasted_iota(jnp.int32, (shape[0], units), 1)
        chosen = jnp.where(unit == column, 1.0, 0.0).astype(BF16)
        for i, weight in enumerate((wg, wu)):
            sel_w[i] = lax.dot_general(
                chosen, weight[...], (((1,), (1,)), ((), ())), preferred_element_type=F32
            ).astype(BF16)

    def a_copy(pair, peer):
        return remote(
            part_a.at[pair, :, peer], got_a.at[t, pair], ra_s.at[pair, peer], ra_r.at[pair, t],
            {"tensor": peer},
        )

    def a_product(pair):
        blocks = 128 // rows
        right = xbuf[pl.ds(pair * blocks, blocks)].reshape(128, width)
        for kind in range(2):
            part = lax.dot_general(
                sel_w[kind], right, (((1,), (1,)), ((), ())), preferred_element_type=F32
            ).astype(BF16)
            for r in range(2 * n_width):
                group = r // n_width
                who = (r + group * n_y) % n_width
                part_a[pair, group, who, kind] = part[r * PICK:(r + 1) * PICK]
        for d in range(1, n_width):
            a_copy(pair, peer_of(d)).start()

    def a_chunk(s):
        here = chip // 2
        k = s // 2
        odd = lax.rem(s, 2) == 1

        @pl.when(odd)
        def _():
            a_product(lax.rem(here + k, n_pair))

        @pl.when(odd & (s > 1))
        def _():
            a_product(wrap(here - k, n_pair))

        @pl.when(s == half)
        def _():
            a_product(lax.rem(here + n_pair // 2, n_pair))

    def a_sum():
        def body(pair, carry):
            for d in range(1, n_width):
                src = peer_of(d)
                ref = got_a.at[src, pair]
                remote(
                    ref, ref, ra_s.at[pair, src], ra_r.at[pair, src], {"tensor": src}
                ).wait_recv()
            return carry

        lax.fori_loop(0, n_pair, body, 0)
        for group in (1, 0):
            pieces = []
            for pair in range(n_pair):
                gate = part_a[pair, group, t, 0].astype(F32)
                up = part_a[pair, group, t, 1].astype(F32)
                for d in range(1, n_width):
                    gate = gate + got_a[peer_of(d), pair, group, 0].astype(F32)
                    up = up + got_a[peer_of(d), pair, group, 1].astype(F32)
                pieces.append(silu_times(gate, up).astype(F32))
            wide = jnp.concatenate(pieces, axis=1)
            mean = jnp.sum(wide, axis=1, keepdims=True) / tokens
            var = jnp.sum(wide * wide, axis=1, keepdims=True) / tokens - mean * mean
            z = ((wide - mean) * lax.rsqrt(var + EPS)).astype(BF16)
            if group == 1:
                cross_z[...] = z
                remote(cross_z, panel.at[dp], cz_s.at[0], cz_r.at[0], other).start()
            else:
                panel[dp] = z

    loads[0].wait()
    ring_start(acts_ring)
    loads[1].wait()
    loads[2].wait()

    @pl.when(is_a)
    def _():
        a_select()

    ring_mate_own(acts_ring)

    def use(s):
        ring_mate(acts_ring, s)

        @pl.when(is_b)
        def _():
            b_product(s)

        @pl.when(is_a)
        def _():
            a_chunk(s)

    owned = [s for s in range(1, half + 1) if s not in helped]
    if half == 8:
        a_early = [(6, raw, 1), (8, take, 2)]
        b_early = [(6, b_pair, 2), (7, b_total, 2), (8, b_pair, 4)]
        a_late = [
            (b_pair, 1), (raw, 3), (b_total, 1), (a_sum,), (panel_start,), (b_pair, 3), (take, 4),
            (b_total, 3), (take, 5), (panel_forward,), (take, 6), (take, 7), (panel_collect,),
            (take, 8),
        ]
        b_late = [
            (b_total, 4), (b_pair, 5), (b_pair, 6), (b_total, 5), (take, 1), (b_pair, 7),
            (b_total, 6), (panel_take_own,), (panel_start,), (b_total, 7), (b_pair, 8), (take, 3),
            (panel_forward,), (b_total, 8), *[(pass_on, s) for s in (2, 4, 5, 1, 6, 7, 3)],
            (panel_collect,),
        ]
    else:
        a_early, b_early = [], []
        a_late = [
            *[(act, s) for s in helped for act in (raw, b_pair, b_total)], (a_sum,), (panel_start,),
            *[(take, s) for s in owned], (panel_forward,), (panel_collect,),
        ]
        b_late = [
            *[(act, s) for s in owned for act in (b_pair, b_total)], (panel_take_own,),
            (panel_start,), *[(take, s) for s in helped], (panel_forward,),
            *[(pass_on, s) for s in range(1, half)], (panel_collect,),
        ]

    def gather_step(s, carry):
        ring_step(acts_ring, s)

        @pl.when(s > 1)
        def _():
            use(s - 1)

        for model, when in ((is_a, a_early), (is_b, b_early)):
            for step, act, chunk in when:
                @pl.when(model & (s == step))
                def _():
                    act(chunk)

        return carry

    lax.fori_loop(1, half + 1, gather_step, 0)
    use(half)

    for model, acts in ((is_a, a_late), (is_b, b_late)):
        @pl.when(model)
        def _():
            for act, *chunk in acts:
                act(*chunk)

    def last(s, carry):
        @pl.when(is_a | (s == half))
        def _():
            ref = hid_b.at[tile_of(s, theirs(s))]
            remote(ref, ref, gx_s.at[s - 1], gx_r.at[s - 1], across).wait_recv()

        return carry

    ring_drain(*acts_ring)
    ring_drain(panel, ((spread, pl.ds(0, PICK)),))
    lax.fori_loop(1, half + 1, last, 0)
    panel_mate()

    def arrive(s, carry):
        for d in range(1, n_y):
            row = y_of(d)
            first = hid_b.at[tile_of(s, mine(s) // n_y * n_y + row)]
            remote(first, first, g1_s.at[s - 1, row], g1_r.at[s - 1, row], at_y(row)).wait_recv()
            second = hid_b.at[tile_of(s, theirs(s) // n_y * n_y + row)]
            remote(second, second, g2_s.at[s - 1, row], g2_r.at[s - 1, row], at_y(row)).wait_recv()
        return carry

    lax.fori_loop(1, half + 1, arrive, 0)

    left = panel[...].reshape(n_data * PICK, tokens)
    scale = 1.0 / math.sqrt(tokens)
    start = 0
    while start < units:
        size = min(256, units - start)
        wide = hid_b[:, :, start:start + size].reshape(tokens, size).astype(F32)
        mean = jnp.sum(wide, axis=0, keepdims=True) / tokens
        var = jnp.sum(wide * wide, axis=0, keepdims=True) / tokens - mean * mean
        z = ((wide - mean) * lax.rsqrt(var + EPS)).astype(BF16)
        score = jnp.dot(left, z, preferred_element_type=F32) * scale
        out_ref[:, start:start + size] = score.astype(BF16)
        start += size

    def sent(s, carry):
        for copy in own_copies(s) + passed_copies(s):
            copy.wait_send()

        @pl.when(is_owner(s))
        def _():
            cross_copy(s, t).wait_send()
            x_copy(s).wait_send()
            for d in range(1, n_y):
                y_copy(s, y_of(d)).wait_send()

        @pl.when(is_b & is_helped(s))
        def _():
            raw_copy(s).wait_send()

        return carry

    lax.fori_loop(1, half + 1, sent, 0)

    @pl.when(is_a)
    def _():
        remote(cross_z, panel.at[dp], cz_s.at[0], cz_r.at[0], other).wait_send()

        def body(pair, carry):
            for d in range(1, n_width):
                a_copy(pair, peer_of(d)).wait_send()
            return carry

        lax.fori_loop(0, n_pair, body, 0)


def body(n_data, n_width, acts, gate_w, up_w, panel_units):
    _, rows, width = acts.shape
    units = gate_w.shape[2]
    tokens = n_data * rows
    steps = n_data // 4
    pairs = n_data // 4
    n_y = n_width // 2
    rings = rows // TILE + 1
    hbm = pl.BlockSpec(memory_space=pltpu.HBM)
    vmem = pl.BlockSpec(memory_space=pltpu.VMEM)
    dma = pltpu.SemaphoreType.DMA
    both = lambda *shape: [dma(shape), dma(shape)]
    return pl.pallas_call(
        functools.partial(kernel, n_data, n_width),
        out_shape=jax.ShapeDtypeStruct((n_data * PICK, units), BF16),
        in_specs=[hbm, hbm, hbm, vmem],
        out_specs=vmem,
        scratch_shapes=[
            pltpu.VMEM((n_data, rows, width), BF16),
            pltpu.VMEM((width, units), BF16),
            pltpu.VMEM((width, units), BF16),
            pltpu.VMEM((steps, n_width, TILE, 2 * units), BF16),
            pltpu.VMEM((steps, n_y, TILE, 2 * units), BF16),
            pltpu.VMEM((steps, n_y, TILE, 2 * units), BF16),
            pltpu.VMEM((steps, n_y, TILE, 2 * units), BF16),
            pltpu.VMEM((tokens // TILE, TILE, units), BF16),
            pltpu.VMEM((2, 2 * n_width * PICK, width), BF16),
            pltpu.VMEM((pairs, 2, n_width, 2, PICK, 128), BF16),
            pltpu.VMEM((n_width, pairs, 2, 2, PICK, 128), BF16),
            pltpu.VMEM((PICK, tokens), BF16),
            pltpu.VMEM((n_data, PICK, tokens), BF16),
            dma((3,)),
            *both(rings, steps + 1),
            *both(rings, steps + 1),
            *both(rings, 2 * steps + 2),
            *both(steps),
            *both(steps),
            *both(steps, n_y),
            *both(steps),
            *both(steps, n_y),
            *both(steps, n_y),
            *both(steps),
            *both(pairs, n_width),
            *both(1),
        ],
        compiler_params=pltpu.CompilerParams(
            collective_id=0, has_side_effects=True, vmem_limit_bytes=62914560
        ),
    )(acts, gate_w, up_w, panel_units.reshape(-1, 128))


def solution(mesh):
    in_specs = (P("mp", "dp", "tensor"), P("mp", "tensor", "dp"), P("mp", "tensor", "dp"), P())
    out_specs = P(("mp", "tensor"), "dp")
    step = functools.partial(body, mesh.shape["dp"], mesh.shape["tensor"])
    return jax.shard_map(step, mesh=mesh, in_specs=in_specs, out_specs=out_specs, check_vma=False)
```

time: 102 us -> 88.2 us (0.86)
  the two profiles are of different devices: /device:TPU:1 before, /device:TPU:6 now
where the time goes in v2:
time: 88.2 us; the launch traced here: 88 us
  Pallas kernels  85.8 us (97%)
  local copies, waits for them, and re-layouts  2.18 us (2%)
    pallas_call x1, Pallas kernels, body(): pl.pallas_call(functools.partial(kernel, n_data, n_width), out_shape=jax....  85.8 us
    unnamed x1, local copies, waits for them, and re-layouts  2.18 us

profile of v2, /device:TPU:6, one launch (start us, length us, event | category | flops | bytes accessed | tf_op | source)
XLA Modules:
  0.0 88.0 jit_solution(17662025550881807078)
XLA Ops:
  0.0 85.8 %shard_map.46 = bf16[512,896]{1,0:T(8,128)(2,1)} custom-call(bf16[1,32,1024]{2,1,0:T(8,128)(2,1)} %acts_ref.1, bf16[1,1024,896]{2,1,0:T(8,128)(2,1)} %gate_ref.1, bf16[1,1024,896]{2,1,0:T(8,128)(2,1)} %up_ref.1, s32[64,128]{1,0:T(8,128)} %bitcast.1), custom_call_target="tpu_custom_call" | custom-call | tf_op jit(solution)/shard_map/pallas_call | solution.py:578
  85.8 2.2 %copy.6 = bf16[512,896]{1,0:T(8,128)(2,1)} copy(bf16[512,896]{1,0:T(8,128)(2,1)} %shard_map.46) | data formatting | bytes 1835008

commit v3 on v2

--- a/solution.py
+++ b/solution.py
@@ -37,9 +37,9 @@
 
 def kernel(
     n_data, n_width, acts_ref, gate_ref, up_ref, table_ref, out_ref,
-    xbuf, wg, wu, part_b, got_x, sum_b, got_y, hid_b, sel_w, part_a, got_a, cross_z, panel,
-    load_sem, up_s, up_r, dn_s, dn_r, pt_s, pt_r, px_s, px_r, rx_s, rx_r, ry_s, ry_r,
-    gx_s, gx_r, g1_s, g1_r, g2_s, g2_r, xc_s, xc_r, ra_s, ra_r, cz_s, cz_r,
+    xbuf, wg, wu, part_b, got_x, sum_b, got_y, got_d, hid_b, sel_w, part_a, got_a, cross_z, panel,
+    load_sem, up_s, up_r, dn_s, dn_r, pt_s, pt_r, px_s, px_r, bk_s, bk_r, rd_s, rd_r, rx_s, rx_r, ry_s, ry_r,
+    gx_s, gx_r, g_s, g_r, xc_s, xc_r, ra_s, ra_r, cz_s, cz_r,
 ):
     mp = lax.axis_index("mp")
     dp = lax.axis_index("dp")
@@ -57,8 +57,6 @@
     width = acts_ref.shape[2]
     units = gate_ref.shape[2]
     tokens = n_data * rows
-    nxt = {"dp": wrap(dp + 2, n_data)}
-    prv = {"dp": wrap(dp - 2, n_data)}
     mate_dp = dp + 1 - 2 * core
     mate = {"dp": mate_dp}
     across_t = lax.rem(t + n_y, n_width)
@@ -72,6 +70,23 @@
     def is_helped(s):
         return functools.reduce(jnp.logical_or, [s == h for h in helped])
 
+    relayed = (1, 2, 4, 5) if half == 8 else ()
+    first_late = 6 if half == 8 else half + 1
+
+    def is_direct(s):
+        passed = functools.reduce(jnp.logical_or, [s == r for r in relayed], s < 0)
+        return jnp.where(is_a, jnp.logical_not(passed), s == half)
+
+    full = [s for s in (2, 4) if s <= half]
+
+    def is_full(s):
+        return functools.reduce(jnp.logical_or, [s == f for f in full])
+
+    returned = [s for s in ((1, 2, 4) if half == 8 else (2,)) if s <= half]
+
+    def is_returned(s):
+        return functools.reduce(jnp.logical_or, [s == r for r in returned])
+
     def is_owner(s):
         return jnp.logical_not(jnp.logical_xor(is_a, is_helped(s)))
 
@@ -100,86 +115,99 @@
 
     barrier = pltpu.get_barrier_semaphore()
     greeted = [mate, other] + [{"tensor": peer_of(d)} for d in range(1, n_width)]
-    for d in range(1, reach + 1):
+    for d in range(1, max(reach, 2) + 1):
         greeted += [{"dp": wrap(dp + 2 * d, n_data)}, {"dp": wrap(dp - 2 * d, n_data)}]
     for device in greeted:
         pl.semaphore_signal(barrier, inc=1, device_id=device, device_id_type=MESH)
     pl.semaphore_wait(barrier, len(greeted))
 
-    sides = ((-2, 0, up_s, up_r, nxt, 0), (2, 1, dn_s, dn_r, prv, 1))
+    sides = ((-2, 0, up_s, up_r, 0), (2, 1, dn_s, dn_r, 1))
     acts_ring = (xbuf, tuple((k, pl.ds(k * TILE, TILE)) for k in range(rows // TILE)))
     spread = rows // TILE
 
+    def away(step, d):
+        return {"dp": wrap(dp - step * d, n_data)}
+
     def ring_start(ring):
         buf, pieces = ring
+        for d in (2, 1):
+            for k, part in pieces:
+                own = buf.at[dp, part]
+                for step, last_core, ss, rs, _odd in sides:
+                    @pl.when((d < half) | (core == last_core))
+                    def _():
+                        remote(own, own, ss.at[k], rs.at[k, d], away(step, d)).start()
         for k, part in pieces:
             own = buf.at[dp, part]
-            for _step, _last, ss, rs, device, _odd in sides:
-                remote(own, own, ss.at[k, 1], rs.at[k, 1], device).start()
-            remote(own, own, pt_s.at[k, 0], pt_r.at[k, 0], mate).start()
+            remote(own, own, pt_s.at[k], pt_r.at[k, 0], mate).start()
 
     def ring_mate_own(ring):
         buf, pieces = ring
         for k, part in pieces:
             theirs = buf.at[mate_dp, part]
-            remote(theirs, theirs, pt_s.at[k, 0], pt_r.at[k, 0], mate).wait_recv()
-
-    def ring_step(ring, s):
+            remote(theirs, theirs, pt_s.at[k], pt_r.at[k, 0], mate).wait_recv()
+
+    def ring_wave(ring, w):
         buf, pieces = ring
-        for k, part in pieces:
-            for step, last_core, ss, rs, device, odd in sides:
-                @pl.when((s < half) | (core == last_core))
-                def _():
-                    ref = buf.at[wrap(dp + step * s, n_data), part]
-                    remote(ref, ref, ss.at[k, s], rs.at[k, s], device).wait_recv()
-
-                    @pl.when((s + 1 < half) | ((s + 1 == half) & (core == last_core)))
+        far = 2 * w
+        for d in (far, far - 1):
+            for k, part in pieces:
+                for step, last_core, ss, rs, odd in sides:
+                    @pl.when((d < half) | (core == last_core))
                     def _():
-                        remote(ref, ref, ss.at[k, s + 1], rs.at[k, s + 1], device).start()
-
-                    slot = 2 * s + odd
-                    remote(ref, ref, pt_s.at[k, slot], pt_r.at[k, slot], mate).start()
+                        ref = buf.at[wrap(dp + step * d, n_data), part]
+                        remote(ref, ref, ss.at[k], rs.at[k, d], mate).wait_recv()
+                        if d is far:
+                            @pl.when((far + 2 < half) | ((far + 2 == half) & (core == last_core)))
+                            def _():
+                                remote(
+                                    ref, ref, ss.at[k], rs.at[k, far + 2], away(step, 2)
+                                ).start()
+
+                            @pl.when(far < half)
+                            def _():
+                                remote(
+                                    ref, ref, ss.at[k], rs.at[k, far + 1], away(step, 1)
+                                ).start()
+
+                        slot = 2 * d + odd
+                        remote(ref, ref, pt_s.at[k], pt_r.at[k, slot], mate).start()
 
     def ring_mate(ring, s):
         buf, pieces = ring
         for k, part in pieces:
-            for step, last_core, _ss, _rs, _device, odd in sides:
+            for step, last_core, _ss, _rs, odd in sides:
                 @pl.when((s < half) | (core != last_core))
                 def _():
                     ref = buf.at[wrap(mate_dp + step * s, n_data), part]
                     slot = 2 * s + odd
-                    remote(ref, ref, pt_s.at[k, slot], pt_r.at[k, slot], mate).wait_recv()
+                    remote(ref, ref, pt_s.at[k], pt_r.at[k, slot], mate).wait_recv()
 
     def ring_drain(buf, pieces):
         for k, part in pieces:
-            own = buf.at[dp, part]
-            remote(own, own, pt_s.at[k, 0], pt_r.at[k, 0], mate).wait_send()
-
-            def body(s, carry):
-                for _step, last_core, ss, rs, device, odd in sides:
-                    @pl.when((s < half) | (core == last_core))
+            everything = buf.at[pl.ds(0, n_chip), part]
+            remote(everything, everything, pt_s.at[k], pt_r.at[k, 0], mate).wait_send()
+            for _step, last_core, ss, rs, _odd in sides:
+                for some, count in ((core == last_core, half), (core != last_core, half - 1)):
+                    @pl.when(some)
                     def _():
-                        slot = 2 * s + odd
-                        remote(own, own, ss.at[k, s], rs.at[k, s], device).wait_send()
-                        remote(own, own, pt_s.at[k, slot], pt_r.at[k, slot], mate).wait_send()
-                return carry
-
-            lax.fori_loop(1, half + 1, body, 0)
+                        ref = buf.at[pl.ds(0, count), part]
+                        remote(ref, ref, ss.at[k], rs.at[k, 1], mate).wait_send()
 
     def panel_start():
         own = panel.at[dp]
         for d in range(reach, 0, -1):
-            for step, _last, ss, rs, _device, _odd in sides:
+            for step, _last, ss, rs, _odd in sides:
                 target = {"dp": wrap(dp - step * d, n_data)}
-                remote(own, own, ss.at[spread, d], rs.at[spread, d], target).start()
-        remote(own, own, pt_s.at[spread, 0], pt_r.at[spread, 0], mate).start()
+                remote(own, own, ss.at[spread], rs.at[spread, d], target).start()
+        remote(own, own, pt_s.at[spread], pt_r.at[spread, 0], mate).start()
 
     def panel_take(d, side):
-        step, _last, ss, rs, device, odd = side
+        step, _last, ss, rs, odd = side
         ref = panel.at[wrap(dp + step * d, n_data)]
-        remote(ref, ref, ss.at[spread, d], rs.at[spread, d], device).wait_recv()
+        remote(ref, ref, ss.at[spread], rs.at[spread, d], mate).wait_recv()
         return ref, remote(
-            ref, ref, pt_s.at[spread, 2 * d + odd], pt_r.at[spread, 2 * d + odd], mate
+            ref, ref, pt_s.at[spread], pt_r.at[spread, 2 * d + odd], mate
         )
 
     def panel_take_own():
@@ -188,12 +216,12 @@
 
     def panel_forward():
         for side in sides:
-            step, last_core, ss, rs, _device, _odd = side
+            step, last_core, ss, rs, _odd = side
             ref, to_mate = panel_take(reach, side)
 
             def pass_to(d):
                 target = {"dp": wrap(dp - step * d, n_data)}
-                return remote(ref, ref, ss.at[spread, reach + d], rs.at[spread, reach + d], target)
+                return remote(ref, ref, ss.at[spread], rs.at[spread, reach + d], target)
 
             @pl.when(core == last_core)
             def _():
@@ -217,16 +245,16 @@
 
     def panel_mate():
         theirs = panel.at[mate_dp]
-        remote(theirs, theirs, pt_s.at[spread, 0], pt_r.at[spread, 0], mate).wait_recv()
+        remote(theirs, theirs, pt_s.at[spread], pt_r.at[spread, 0], mate).wait_recv()
 
         def body(d, carry):
-            for step, last_core, _ss, _rs, _device, odd in sides:
+            for step, last_core, _ss, _rs, odd in sides:
                 @pl.when((d < half) | (core != last_core))
                 def _():
                     ref = panel.at[wrap(mate_dp + step * d, n_data)]
                     slot = 2 * d + odd
                     remote(
-                        ref, ref, pt_s.at[spread, slot], pt_r.at[spread, slot], mate
+                        ref, ref, pt_s.at[spread], pt_r.at[spread, slot], mate
                     ).wait_recv()
             return carry
 
@@ -241,13 +269,13 @@
         copies = [remote(ref, ref, gx_s.at[s - 1], gx_r.at[s - 1], across)]
         for d in range(1, n_y):
             row = y_of(d)
-            copies.append(remote(ref, ref, g1_s.at[s - 1, row], g1_r.at[s - 1, y], at_y(row)))
+            copies.append(remote(ref, ref, g_s.at[s - 1], g_r.at[s - 1], at_y(row)))
         return copies
 
     def passed_copies(s):
         ref = hid_b.at[tile_of(s, theirs(s))]
         return [
-            remote(ref, ref, g2_s.at[s - 1, y_of(d)], g2_r.at[s - 1, y], at_y(y_of(d)))
+            remote(ref, ref, g_s.at[s - 1], g_r.at[s - 1], at_y(y_of(d)))
             for d in range(1, n_y)
         ]
 
@@ -255,7 +283,7 @@
         ref = hid_b.at[tile_of(s, mine(s))]
         return [
             remote(
-                ref, ref, g2_s.at[s - 1, y_of(d)], g2_r.at[s - 1, y],
+                ref, ref, g_s.at[s - 1], g_r.at[s - 1],
                 {"tensor": (1 - x) * n_y + y_of(d)},
             )
             for d in range(1, n_y)
@@ -281,13 +309,32 @@
         ref = part_b.at[s - 1]
         return remote(ref, ref, px_s.at[s - 1], px_r.at[s - 1], other)
 
+    def full_copy(s, peer):
+        k = s // 2 - 1
+        return remote(
+            part_b.at[s - 1, peer], got_d.at[k, t], rd_s.at[k], rd_r.at[k], {"tensor": peer}
+        )
+
+    def full_total(s):
+        k = s // 2 - 1
+        total = part_b[s - 1, t].astype(F32)
+        seven = got_d.at[k, pl.ds(0, n_width - 1)]
+        remote(seven, seven, rd_s.at[k], rd_r.at[k], across).wait_recv()
+        for d in range(1, n_width):
+            src = peer_of(d)
+            total = total + got_d[k, src].astype(F32)
+        finish(s, total)
+
+    def start_x(s):
+        x_copy(s).start()
+
     def raw(s):
         raw_copy(s).wait_recv()
         x_copy(s).start()
 
     def y_copy(s, row):
         return remote(
-            sum_b.at[s - 1, row], got_y.at[s - 1, y], ry_s.at[s - 1, row], ry_r.at[s - 1, y], at_y(row)
+            sum_b.at[s - 1, row], got_y.at[s - 1, y], ry_s.at[s - 1], ry_r.at[s - 1], at_y(row)
         )
 
     def b_product(s):
@@ -302,9 +349,14 @@
         def _():
             raw_copy(s).start()
 
-        @pl.when(jnp.logical_not(is_helped(s)))
-        def _():
-            x_copy(s).start()
+        @pl.when(is_full(s))
+        def _():
+            for d in range(1, n_width):
+                full_copy(s, peer_of(d)).start()
+
+        @pl.when(jnp.logical_not(is_helped(s) | is_full(s)) & (s < first_late))
+        def _():
+            start_x(s)
 
     def b_pair(s):
         x_copy(s).wait_recv()
@@ -316,23 +368,60 @@
 
     def b_total(s):
         total = part_b[s - 1, t].astype(F32) + got_x[s - 1, y].astype(F32)
+        three = got_y.at[s - 1, pl.ds(0, n_y - 1)]
+        remote(three, three, ry_s.at[s - 1], ry_r.at[s - 1], across).wait_recv()
         for d in range(1, n_y):
             row = y_of(d)
-            ref = got_y.at[s - 1, row]
-            remote(ref, ref, ry_s.at[s - 1, row], ry_r.at[s - 1, row], at_y(row)).wait_recv()
             total = total + got_y[s - 1, row].astype(F32)
+        finish(s, total)
+
+    def finish(s, total):
         hid_b[tile_of(s, t)] = silu_times(total[:, :units], total[:, units:])
         cross_copy(s, t).start()
         share(s)
 
     def share(s):
-        for copy in own_copies(s):
+        @pl.when(is_a | (s not in returned))
+        def _():
+            for copy in own_copies(s):
+                copy.start()
+
+            @pl.when(is_direct(s))
+            def _():
+                for copy in direct_copies(s):
+                    copy.start()
+
+    def back_copies(s):
+        k = returned.index(s)
+        copies = []
+        for d in range(1, n_width):
+            who = lax.rem(mine(s) + d, n_width)
+            ref = hid_b.at[tile_of(s, who)]
+            copies.append(remote(ref, ref, bk_s.at[k], bk_r.at[k], other))
+        return copies
+
+    def wait_x(s):
+        ref = hid_b.at[tile_of(s, theirs(s))]
+        remote(ref, ref, gx_s.at[s - 1], gx_r.at[s - 1], across).wait_recv()
+
+    def six_tiles(s):
+        six = hid_b.at[pl.ds(0, 2 * n_y - 2)]
+        return remote(six, six, g_s.at[s - 1], g_r.at[s - 1], across)
+
+    def wait_y(s):
+        six_tiles(s).wait_recv()
+
+    def seven_tiles(s):
+        k = returned.index(s)
+        seven = hid_b.at[pl.ds(0, n_width - 1)]
+        return remote(seven, seven, bk_s.at[k], bk_r.at[k], other)
+
+    def give_back(s):
+        if s not in relayed:
+            wait_x(s)
+        wait_y(s)
+        for copy in back_copies(s):
             copy.start()
-
-        @pl.when(is_a | (s == half))
-        def _():
-            for copy in direct_copies(s):
-                copy.start()
 
     def take(s):
         cross_copy(s, mine(s)).wait_recv()
@@ -357,7 +446,7 @@
 
     def a_copy(pair, peer):
         return remote(
-            part_a.at[pair, :, peer], got_a.at[t, pair], ra_s.at[pair, peer], ra_r.at[pair, t],
+            part_a.at[pair, :, peer], got_a.at[t, pair], ra_s.at[0], ra_r.at[0],
             {"tensor": peer},
         )
 
@@ -393,16 +482,8 @@
             a_product(lax.rem(here + n_pair // 2, n_pair))
 
     def a_sum():
-        def body(pair, carry):
-            for d in range(1, n_width):
-                src = peer_of(d)
-                ref = got_a.at[src, pair]
-                remote(
-                    ref, ref, ra_s.at[pair, src], ra_r.at[pair, src], {"tensor": src}
-                ).wait_recv()
-            return carry
-
-        lax.fori_loop(0, n_pair, body, 0)
+        others = got_a.at[pl.ds(0, n_width - 1)]
+        remote(others, others, ra_s.at[0], ra_r.at[0], across).wait_recv()
         for group in (1, 0):
             pieces = []
             for pair in range(n_pair):
@@ -446,47 +527,44 @@
 
     owned = [s for s in range(1, half + 1) if s not in helped]
     if half == 8:
-        a_early = [(6, raw, 1), (8, take, 2)]
-        b_early = [(6, b_pair, 2), (7, b_total, 2), (8, b_pair, 4)]
         a_late = [
-            (b_pair, 1), (raw, 3), (b_total, 1), (a_sum,), (panel_start,), (b_pair, 3), (take, 4),
-            (b_total, 3), (take, 5), (panel_forward,), (take, 6), (take, 7), (panel_collect,),
-            (take, 8),
+            (raw, 1), (a_sum,), (panel_start,), (take, 2), (raw, 3), (b_pair, 1), (take, 4),
+            (pass_on, 2), (b_total, 1), (pass_on, 4), (b_pair, 3), (give_back, 2), (panel_forward,),
+            (take, 5), (pass_on, 1), (b_total, 3), (take, 6), (take, 7), (give_back, 4),
+            (pass_on, 5), (panel_collect,), (give_back, 1), (take, 8),
         ]
         b_late = [
-            (b_total, 4), (b_pair, 5), (b_pair, 6), (b_total, 5), (take, 1), (b_pair, 7),
-            (b_total, 6), (panel_take_own,), (panel_start,), (b_total, 7), (b_pair, 8), (take, 3),
-            (panel_forward,), (b_total, 8), *[(pass_on, s) for s in (2, 4, 5, 1, 6, 7, 3)],
+            (full_total, 2), (full_total, 4), (start_x, 6), (b_pair, 5), (start_x, 7),
+            (panel_take_own,), (panel_start,), (b_total, 5), (b_pair, 6), (start_x, 8),
+            (panel_forward,), (b_pair, 7), (b_total, 6), (take, 1), (b_total, 7), (b_pair, 8),
+            (pass_on, 5), (pass_on, 6), (pass_on, 7), (b_total, 8), (take, 3), (pass_on, 3),
             (panel_collect,),
         ]
     else:
-        a_early, b_early = [], []
         a_late = [
             *[(act, s) for s in helped for act in (raw, b_pair, b_total)], (a_sum,), (panel_start,),
-            *[(take, s) for s in owned], (panel_forward,), (panel_collect,),
+            *[(take, s) for s in owned], (panel_forward,), *[(give_back, s) for s in returned],
+            (panel_collect,),
         ]
         b_late = [
-            *[(act, s) for s in owned for act in (b_pair, b_total)], (panel_take_own,),
+            *[(full_total, s) for s in owned if s in full],
+            *[(act, s) for s in owned if s not in full for act in (b_pair, b_total)],
+            (panel_take_own,),
             (panel_start,), *[(take, s) for s in helped], (panel_forward,),
             *[(pass_on, s) for s in range(1, half)], (panel_collect,),
         ]
 
-    def gather_step(s, carry):
-        ring_step(acts_ring, s)
-
-        @pl.when(s > 1)
-        def _():
-            use(s - 1)
-
-        for model, when in ((is_a, a_early), (is_b, b_early)):
-            for step, act, chunk in when:
-                @pl.when(model & (s == step))
-                def _():
-                    act(chunk)
-
+    def gather_wave(w, carry):
+        ring_wave(acts_ring, w)
+
+        @pl.when(w > 1)
+        def _():
+            use(2 * w - 2)
+
+        use(2 * w - 1)
         return carry
 
-    lax.fori_loop(1, half + 1, gather_step, 0)
+    lax.fori_loop(1, half // 2 + 1, gather_wave, 0)
     use(half)
 
     for model, acts in ((is_a, a_late), (is_b, b_late)):
@@ -496,10 +574,9 @@
                 act(*chunk)
 
     def last(s, carry):
-        @pl.when(is_a | (s == half))
-        def _():
-            ref = hid_b.at[tile_of(s, theirs(s))]
-            remote(ref, ref, gx_s.at[s - 1], gx_r.at[s - 1], across).wait_recv()
+        @pl.when(is_direct(s) & jnp.logical_not(is_returned(s)))
+        def _():
+            wait_x(s)
 
         return carry
 
@@ -509,13 +586,16 @@
     panel_mate()
 
     def arrive(s, carry):
-        for d in range(1, n_y):
-            row = y_of(d)
-            first = hid_b.at[tile_of(s, mine(s) // n_y * n_y + row)]
-            remote(first, first, g1_s.at[s - 1, row], g1_r.at[s - 1, row], at_y(row)).wait_recv()
-            second = hid_b.at[tile_of(s, theirs(s) // n_y * n_y + row)]
-            remote(second, second, g2_s.at[s - 1, row], g2_r.at[s - 1, row], at_y(row)).wait_recv()
+        @pl.when(jnp.logical_not(is_returned(s)))
+        def _():
+            wait_y(s)
+
         return carry
+
+    @pl.when(is_b)
+    def _():
+        for s in returned:
+            seven_tiles(s).wait_recv()
 
     lax.fori_loop(1, half + 1, arrive, 0)
 
@@ -533,15 +613,26 @@
         start += size
 
     def sent(s, carry):
-        for copy in own_copies(s) + passed_copies(s):
-            copy.wait_send()
+        @pl.when(is_a | jnp.logical_not(is_returned(s)))
+        def _():
+            own_copies(s)[0].wait_send()
+            six_tiles(s).wait_send()
 
         @pl.when(is_owner(s))
         def _():
             cross_copy(s, t).wait_send()
-            x_copy(s).wait_send()
-            for d in range(1, n_y):
-                y_copy(s, y_of(d)).wait_send()
+
+            @pl.when(is_full(s))
+            def _():
+                k = s // 2 - 1
+                seven = part_b.at[s - 1, pl.ds(0, n_width - 1)]
+                remote(seven, seven, rd_s.at[k], rd_r.at[k], across).wait_send()
+
+            @pl.when(jnp.logical_not(is_full(s)))
+            def _():
+                x_copy(s).wait_send()
+                three = sum_b.at[s - 1, pl.ds(0, n_y - 1)]
+                remote(three, three, ry_s.at[s - 1], ry_r.at[s - 1], across).wait_send()
 
         @pl.when(is_b & is_helped(s))
         def _():
@@ -554,13 +645,11 @@
     @pl.when(is_a)
     def _():
         remote(cross_z, panel.at[dp], cz_s.at[0], cz_r.at[0], other).wait_send()
-
-        def body(pair, carry):
-            for d in range(1, n_width):
-                a_copy(pair, peer_of(d)).wait_send()
-            return carry
-
-        lax.fori_loop(0, n_pair, body, 0)
+        for s in returned:
+            seven_tiles(s).wait_send()
+
+        others = part_a.at[:, :, pl.ds(0, n_width - 1)]
+        remote(others, others, ra_s.at[0], ra_r.at[0], across).wait_send()
 
 
 def body(n_data, n_width, acts, gate_w, up_w, panel_units):
@@ -588,6 +677,7 @@
             pltpu.VMEM((steps, n_y, TILE, 2 * units), BF16),
             pltpu.VMEM((steps, n_y, TILE, 2 * units), BF16),
             pltpu.VMEM((steps, n_y, TILE, 2 * units), BF16),
+            pltpu.VMEM((2, n_width, TILE, 2 * units), BF16),
             pltpu.VMEM((tokens // TILE, TILE, units), BF16),
             pltpu.VMEM((2, 2 * n_width * PICK, width), BF16),
             pltpu.VMEM((pairs, 2, n_width, 2, PICK, 128), BF16),
@@ -595,17 +685,21 @@
             pltpu.VMEM((PICK, tokens), BF16),
             pltpu.VMEM((n_data, PICK, tokens), BF16),
             dma((3,)),
-            *both(rings, steps + 1),
-            *both(rings, steps + 1),
-            *both(rings, 2 * steps + 2),
+            dma((rings,)),
+            dma((rings, steps + 1)),
+            dma((rings,)),
+            dma((rings, steps + 1)),
+            dma((rings,)),
+            dma((rings, 2 * steps + 2)),
+            *both(steps),
+            *both(3),
+            *both(2),
             *both(steps),
             *both(steps),
-            *both(steps, n_y),
             *both(steps),
-            *both(steps, n_y),
-            *both(steps, n_y),
             *both(steps),
-            *both(pairs, n_width),
+            *both(steps),
+            *both(1),
             *both(1),
         ],
         compiler_params=pltpu.CompilerParams(

time: 88.2 us -> 81.8 us (0.927)
  the two profiles are of different devices: /device:TPU:6 before, /device:TPU:1 now
where the time goes in v3:
time: 81.8 us; the launch traced here: 81.6 us
  Pallas kernels  79.4 us (97%)
  local copies, waits for them, and re-layouts  2.18 us (3%)
    pallas_call x1, Pallas kernels, body(): pl.pallas_call(functools.partial(kernel, n_data, n_width), out_shape=jax....  79.4 us
    unnamed x1, local copies, waits for them, and re-layouts  2.18 us

profile of v3, /device:TPU:1, one launch (start us, length us, event | category | flops | bytes accessed | tf_op | source)
XLA Modules:
  0.0 81.6 jit_solution(4997602798999128989)
XLA Ops:
  0.0 79.4 %shard_map.46 = bf16[512,896]{1,0:T(8,128)(2,1)} custom-call(bf16[1,32,1024]{2,1,0:T(8,128)(2,1)} %acts_ref.1, bf16[1,1024,896]{2,1,0:T(8,128)(2,1)} %gate_ref.1, bf16[1,1024,896]{2,1,0:T(8,128)(2,1)} %up_ref.1, s32[64,128]{1,0:T(8,128)} %bitcast.1), custom_call_target="tpu_custom_call" | custom-call | tf_op jit(solution)/shard_map/pallas_call | solution.py:667
  79.4 2.2 %copy.6 = bf16[512,896]{1,0:T(8,128)(2,1)} copy(bf16[512,896]{1,0:T(8,128)(2,1)} %shard_map.46) | data formatting | bytes 1835008

commit v4 on v3

--- a/solution.py
+++ b/solution.py
@@ -39,7 +39,7 @@
     n_data, n_width, acts_ref, gate_ref, up_ref, table_ref, out_ref,
     xbuf, wg, wu, part_b, got_x, sum_b, got_y, got_d, hid_b, sel_w, part_a, got_a, cross_z, panel,
     load_sem, up_s, up_r, dn_s, dn_r, pt_s, pt_r, px_s, px_r, bk_s, bk_r, rd_s, rd_r, rx_s, rx_r, ry_s, ry_r,
-    gx_s, gx_r, g_s, g_r, xc_s, xc_r, ra_s, ra_r, cz_s, cz_r,
+    gx_r, g_s, g_r, xc_s, xc_r, ra_s, ra_r, cz_s, cz_r,
 ):
     mp = lax.axis_index("mp")
     dp = lax.axis_index("dp")
@@ -266,7 +266,7 @@
 
     def own_copies(s):
         ref = hid_b.at[tile_of(s, mine(s))]
-        copies = [remote(ref, ref, gx_s.at[s - 1], gx_r.at[s - 1], across)]
+        copies = [remote(ref, ref, g_s.at[s - 1], gx_r.at[s - 1], across)]
         for d in range(1, n_y):
             row = y_of(d)
             copies.append(remote(ref, ref, g_s.at[s - 1], g_r.at[s - 1], at_y(row)))
@@ -295,7 +295,7 @@
 
     def pass_on(s):
         ref = hid_b.at[tile_of(s, theirs(s))]
-        remote(ref, ref, gx_s.at[s - 1], gx_r.at[s - 1], across).wait_recv()
+        remote(ref, ref, g_s.at[s - 1], gx_r.at[s - 1], across).wait_recv()
         for copy in passed_copies(s):
             copy.start()
 
@@ -307,7 +307,7 @@
 
     def raw_copy(s):
         ref = part_b.at[s - 1]
-        return remote(ref, ref, px_s.at[s - 1], px_r.at[s - 1], other)
+        return remote(ref, ref, px_s.at[s // 2], px_r.at[s // 2], other)
 
     def full_copy(s, peer):
         k = s // 2 - 1
@@ -402,7 +402,7 @@
 
     def wait_x(s):
         ref = hid_b.at[tile_of(s, theirs(s))]
-        remote(ref, ref, gx_s.at[s - 1], gx_r.at[s - 1], across).wait_recv()
+        remote(ref, ref, g_s.at[s - 1], gx_r.at[s - 1], across).wait_recv()
 
     def six_tiles(s):
         six = hid_b.at[pl.ds(0, 2 * n_y - 2)]
@@ -615,8 +615,8 @@
     def sent(s, carry):
         @pl.when(is_a | jnp.logical_not(is_returned(s)))
         def _():
-            own_copies(s)[0].wait_send()
-            six_tiles(s).wait_send()
+            sent_tiles = hid_b.at[pl.ds(0, n_width - 1)]
+            remote(sent_tiles, sent_tiles, g_s.at[s - 1], g_r.at[s - 1], across).wait_send()
 
         @pl.when(is_owner(s))
         def _():
@@ -691,12 +691,12 @@
             dma((rings, steps + 1)),
             dma((rings,)),
             dma((rings, 2 * steps + 2)),
-            *both(steps),
+            *both(2),
             *both(3),
             *both(2),
             *both(steps),
             *both(steps),
-            *both(steps),
+            dma((steps,)),
             *both(steps),
             *both(steps),
             *both(1),

time: 81.8 us -> 81.6 us (level)
  no operation moved by 1% of the time
where the time goes in v4:
time: 81.6 us; the launch traced here: 81.4 us
  Pallas kernels  79.2 us (97%)
  local copies, waits for them, and re-layouts  2.18 us (3%)
    pallas_call x1, Pallas kernels, body(): pl.pallas_call(functools.partial(kernel, n_data, n_width), out_shape=jax....  79.2 us
    unnamed x1, local copies, waits for them, and re-layouts  2.18 us

profile of v4, /device:TPU:1, one launch (start us, length us, event | category | flops | bytes accessed | tf_op | source)
XLA Modules:
  0.0 81.4 jit_solution(5479349149203484445)
XLA Ops:
  0.0 79.2 %shard_map.46 = bf16[512,896]{1,0:T(8,128)(2,1)} custom-call(bf16[1,32,1024]{2,1,0:T(8,128)(2,1)} %acts_ref.1, bf16[1,1024,896]{2,1,0:T(8,128)(2,1)} %gate_ref.1, bf16[1,1024,896]{2,1,0:T(8,128)(2,1)} %up_ref.1, s32[64,128]{1,0:T(8,128)} %bitcast.1), custom_call_target="tpu_custom_call" | custom-call | tf_op jit(solution)/shard_map/pallas_call | solution.py:667
  79.2 2.2 %copy.6 = bf16[512,896]{1,0:T(8,128)(2,1)} copy(bf16[512,896]{1,0:T(8,128)(2,1)} %shard_map.46) | data formatting | bytes 1835008
